TPU v7x, 256 devices: a whole 4x4x8 slice. The times are simulated.
256 devices in a mesh: dp: 16 (over z, core), expert: 16 (over y, x).
Axes of the slice: x: 4, y: 4, z: 8, core: 2. Of those that a mesh axis runs over, the one named last changes fastest.
Arguments:
- tokens: bfloat16 [32768, 2048], P(('dp', 'expert')), may hold values from -6 to 6
- out_grad: bfloat16 [32768, 2048], P(('dp', 'expert')), may hold values from -1.5 to 1.5
- routes: int32 [32768, 2], P(('dp', 'expert')), may hold values from 0 to 15, all different within a row; in each aligned block of 128 rows (0 to 127, 128 to 255, ...) at most 32 rows name the same one
- route_probs: bfloat16 [32768, 2], P(('dp', 'expert')), may hold values from 0.049804688 to 1
- kept_count: int32 [16], P('dp'), may hold values from 512 to 2048, as said below
- gate_weight: bfloat16 [16, 2048, 768], P('expert', 'dp'), may hold values from -0.125 to 0.125
- up_weight: bfloat16 [16, 2048, 768], P('expert', 'dp'), may hold values from -0.125 to 0.125
- down_weight: bfloat16 [16, 2048, 768], P('expert', 'dp'), may hold values from -0.21875 to 0.21875
Outputs:
- token_grad: bfloat16 [32768, 2048], P(('dp', 'expert'))
- prob_grad: bfloat16 [32768, 2], P(('dp', 'expert'))
- weight_grad: bfloat16 [16, 2048, 2304], P('expert', 'dp')
Inputs may be any that keep to these rules, and one draw needn't show every extreme that they name: `routes`: among the rows of one device, no expert is named more than 32 times, and a row names 2 different experts. `kept_count`: rows of a data group whose index within the group is below its count are kept; in every draw some group keeps all its rows and another keeps a quarter of them.
All inputs are finite; a program needn't handle non-finite values.
Results may differ from a plain program's by a relative error of at most 0.018.
Values may be sent and summed in bfloat16 or wider, within the bound.
No kernel may reach another device: no remote copies, remote signals or barrier semaphores. Data moves between devices by JAX's collectives and lax.ppermute only.
A program may use at most 128 MiB of HBM per device.

v0:
```python
import jax
import jax.numpy as jnp
from jax import lax
from jax.sharding import PartitionSpec as P


def contract_rows(left, right):
    return lax.dot_general(
        left, right, (((0,), (0,)), ((), ())), preferred_element_type=jnp.float32
    )


def contract_last(left, right):
    return lax.dot_general(
        left, right, (((1,), (1,)), ((), ())), preferred_element_type=jnp.float32
    )


def per_device(
    tokens, out_grad, routes, route_probs, kept_count, gate_weight, up_weight, down_weight
):
    tok_rows, width = tokens.shape
    top = routes.shape[1]
    experts = lax.axis_size("expert")
    capacity = 2 * tok_rows * top // experts
    slots = experts * capacity
    gate_local = gate_weight[0]
    up_local = up_weight[0]
    down_local = down_weight[0]
    row = lax.axis_index("expert") * tok_rows + jnp.arange(tok_rows, dtype=jnp.int32)
    kept = row < kept_count[0]
    masked = jnp.where(kept[:, None], out_grad, jnp.zeros_like(out_grad))
    flat = routes.reshape(-1)
    onehot = (flat[:, None] == jnp.arange(experts, dtype=jnp.int32)[None, :]).astype(jnp.int32)
    before = jnp.cumsum(onehot, axis=0) - onehot
    position = jnp.sum(before * onehot, axis=1)
    target = (flat * capacity + position).reshape(tok_rows, top)
    match = target[None, :, :] == jnp.arange(slots, dtype=jnp.int32)[:, None, None]
    placing = jnp.any(match, axis=2).astype(jnp.bfloat16)
    send_rows = jnp.dot(placing, tokens, preferred_element_type=jnp.float32).astype(jnp.bfloat16)
    send_grad = jnp.dot(placing, masked, preferred_element_type=jnp.float32).astype(jnp.bfloat16)
    send_prob = jnp.sum(
        jnp.where(match, route_probs[None, :, :].astype(jnp.float32), 0.0), axis=(1, 2)
    ).astype(jnp.bfloat16)
    rows_in, grad_in, prob_in = (
        lax.all_to_all(send_rows, "expert", split_axis=0, concat_axis=0, tiled=True),
        lax.all_to_all(send_grad, "expert", split_axis=0, concat_axis=0, tiled=True),
        lax.all_to_all(send_prob, "expert", split_axis=0, concat_axis=0, tiled=True),
    )
    pieces = (
        lax.all_gather(gate_local, "dp", axis=0, tiled=True),
        lax.all_gather(up_local, "dp", axis=0, tiled=True),
    )
    pre_gate = jnp.dot(rows_in, pieces[0], preferred_element_type=jnp.float32)
    pre_up = jnp.dot(rows_in, pieces[1], preferred_element_type=jnp.float32)
    sig = jax.nn.sigmoid(pre_gate)
    act = (pre_gate * sig * pre_up).astype(jnp.bfloat16)
    scaled = (prob_in.astype(jnp.float32)[:, None] * grad_in.astype(jnp.float32)).astype(
        jnp.bfloat16
    )
    piece = lax.all_gather(down_local, "dp", axis=0, tiled=True)
    scaled_part = scaled
    output_part = contract_last(act, piece)
    back_hidden = jnp.dot(scaled_part, piece, preferred_element_type=jnp.float32)
    prob_part = jnp.sum(grad_in.astype(jnp.float32) * output_part, axis=1)
    d_gate = (back_hidden * pre_up * sig * (1.0 + pre_gate * (1.0 - sig))).astype(jnp.bfloat16)
    d_up = (back_hidden * pre_gate * sig).astype(jnp.bfloat16)
    stacked = jnp.stack((gate_local, up_local))
    pieces = lax.all_gather(stacked, "dp", axis=1, tiled=True)
    route_back = (contract_last(d_gate, pieces[0]) + contract_last(d_up, pieces[1])).astype(
        jnp.bfloat16
    )
    scaled_part = scaled
    summed = lax.psum_scatter(
        jnp.concatenate(
            (
                contract_rows(rows_in, d_gate),
                contract_rows(rows_in, d_up),
                contract_rows(scaled_part, act),
            ),
            axis=1,
        ).astype(jnp.bfloat16),
        "dp",
        scatter_dimension=0,
        tiled=True,
    )
    weight_grad = summed[None]
    rows_back, prob_back = (
        lax.all_to_all(route_back, "expert", split_axis=0, concat_axis=0, tiled=True),
        lax.all_to_all(
            prob_part.astype(jnp.bfloat16), "expert", split_axis=0, concat_axis=0, tiled=True
        ),
    )
    token_grad = contract_rows(placing, rows_back).astype(jnp.bfloat16)
    prob_grad = jnp.sum(
        jnp.where(match, prob_back.astype(jnp.float32)[:, None, None], 0.0), axis=0
    ).astype(jnp.bfloat16)
    return (token_grad, prob_grad, weight_grad)


def solution(mesh):
    in_specs = (
        P(("dp", "expert"), None),
        P(("dp", "expert"), None),
        P(("dp", "expert"), None),
        P(("dp", "expert"), None),
        P("dp"),
        P("expert", "dp", None),
        P("expert", "dp", None),
        P("expert", "dp", None),
    )
    out_specs = (P(("dp", "expert"), None), P(("dp", "expert"), None), P("expert", "dp", None))
    return jax.shard_map(
        per_device, mesh=mesh, in_specs=in_specs, out_specs=out_specs, check_vma=False
    )
```

profile of v0, /device:TPU:2, one launch (start us, length us, event | category | flops | bytes accessed | tf_op | source)
XLA Modules:
  0.0 271.1 jit_solution(16039769534471107603)
XLA Ops:
  9.5 1.8 pad_maximum_fusion.1
  13.6 2.0 convolution_convert_fusion.3
  15.6 7.6 %all-to-all-start.2 = ((bf16[16,32,2048]{2,1,0:T(8,128)(2,1)}), bf16[16,32,2048]{2,1,0:T(8,128)(2,1)S(1)}, u32[]{:S(2)}, u32[]{:S(2)}) async-start(bf16[16,32,2048]{2,1,0:T(8,128)(2,1)} %bitcast.5), calls=%async_computation.2 | async-start | bytes 4194304 | tf_op jit(solution)/shard_map/all_to_all | solution.py:46
  23.9 2.2 convolution_convert_fusion.4
  26.1 24.3 %all-to-all-done.2 = bf16[16,32,2048]{2,1,0:T(8,128)(2,1)S(1)} async-done(((bf16[16,32,2048]{2,1,0:T(8,128)(2,1)}), bf16[16,32,2048]{2,1,0:T(8,128)(2,1)S(1)}, u32[]{:S(2)}, u32[]{:S(2)}) %all-to-all-start.2) | async-done | bytes 2097184 | tf_op jit(solution)/shard_map/all_to_all | solution.py:46
  51.7 8.1 %all-to-all-start.1 = ((bf16[16,32,2048]{2,1,0:T(8,128)(2,1)}), bf16[16,32,2048]{2,1,0:T(8,128)(2,1)S(1)}, u32[]{:S(2)}, u32[]{:S(2)}) async-start(bf16[16,32,2048]{2,1,0:T(8,128)(2,1)} %bitcast.72), calls=%async_computation.1 | async-start | bytes 4194304 | tf_op jit(solution)/shard_map/all_to_all | solution.py:47
  59.8 5.5 %fusion.4 = f32[512,768]{1,0:T(8,128)} fusion(bf16[512,2048]{1,0:T(8,128)(2,1)} %bitcast.75, bf16[1,2048,768]{2,1,0:T(8,128)(2,1)} %all-gather.14.cloned.1.call-done), kind=kOutput, calls=%fused_computation.13 | convolution fusion | flops 1610612736 | bytes 6815744 | tf_op jit(solution)/shard_map/dot_general | solution.py:54
  65.3 30.2 %all-gather.12.cloned.1.call-done = bf16[1,2048,768]{2,1,0:T(8,128)(2,1)} async-done(((bf16[1,128,768]{2,1,0:T(8,128)(2,1)}), bf16[1,2048,768]{2,1,0:T(8,128)(2,1)}) %all-gather.12.cloned.1.call-update) | async-done | bytes 3145744 | tf_op jit(solution)/shard_map/all_gather | solution.py:52
  95.5 5.9 %multiply_convert_fusion = (bf16[512,768]{1,0:T(8,128)(2,1)S(1)}, f32[512,768]{1,0:T(8,128)}) fusion(f32[512,768]{1,0:T(8,128)} %fusion.4, bf16[512,2048]{1,0:T(8,128)(2,1)} %bitcast.76, bf16[1,2048,768]{2,1,0:T(8,128)(2,1)} %all-gather.12.cloned.1.call-done), kind=kOutput, calls=%fused_computation.23 | convolution fusion | flops 1612972032 | bytes 9175040 | tf_op jit(solution)/shard_map/dot_general | solution.py:55
  101.4 35.5 %all-gather.10.cloned.1.call-done = bf16[1,2048,768]{2,1,0:T(8,128)(2,1)} async-done(((bf16[1,128,768]{2,1,0:T(8,128)(2,1)}), bf16[1,2048,768]{2,1,0:T(8,128)(2,1)}) %all-gather.10.cloned.1.call-update) | async-done | bytes 3145744 | tf_op jit(solution)/shard_map/all_gather | solution.py:61
  137.0 3.8 %fusion.1 = bf16[512]{0:T(512)(128)(2,1)S(1)} fusion(bf16[512,2048]{1,0:T(8,128)(2,1)S(1)} %bitcast.71, bf16[512,768]{1,0:T(8,128)(2,1)S(1)} %get-tuple-element.22, bf16[1,2048,768]{2,1,0:T(8,128)(2,1)} %all-gather.10.cloned.1.call-done), kind=kOutput, calls=%fused_computation.4 | convolution fusion | flops 1613757952 | bytes 6030336 | tf_op jit(solution)/shard_map/dot_general | solution.py:14
  141.5 7.3 %all-to-all-start.4 = ((bf16[16,32,1]{1,2,0:T(2,128)(2,1)}), bf16[16,32,1]{1,2,0:T(2,128)(2,1)S(1)}, u32[]{:S(2)}, u32[]{:S(2)}) async-start(bf16[16,32,1]{1,2,0:T(2,128)(2,1)} %convert_element_type.119), calls=%async_computation.4 | async-start | bytes 16384 | tf_op jit(solution)/shard_map/all_to_all | solution.py:90
  148.8 6.1 %all-to-all-done.4 = bf16[16,32,1]{1,2,0:T(2,128)(2,1)S(1)} async-done(((bf16[16,32,1]{1,2,0:T(2,128)(2,1)}), bf16[16,32,1]{1,2,0:T(2,128)(2,1)S(1)}, u32[]{:S(2)}, u32[]{:S(2)}) %all-to-all-start.4) | async-done | bytes 1056 | tf_op jit(solution)/shard_map/all_to_all | solution.py:90
  155.8 10.5 %all_to_all.45 = bf16[16,32,1]{1,2,0:T(2,128)(2,1)S(1)} all-to-all(bf16[16,32,1]{1,2,0:T(2,128)(2,1)S(1)} %convert_element_type.118), channel_id=1, replica_groups=mesh['dp'=16,'expert'=16] {'expert'}, dimensions={0} | all-to-all | bytes 2048 | tf_op jit(solution)/shard_map/all_to_all | solution.py:48
  166.9 1.9 convolution_convert_fusion
  169.8 2.1 multiply_convert_fusion.2
  171.9 1.9 convolution_convert_fusion.1
  173.8 1.9 convolution_convert_fusion.2
  175.7 4.5 %pad_maximum_fusion = bf16[2048,2304]{0,1:T(8,128)(2,1)} fusion(bf16[2048,768]{0,1:T(8,128)(2,1)S(1)} %convolution_convert_fusion, bf16[2048,768]{0,1:T(8,128)(2,1)S(1)} %convolution_convert_fusion.1, bf16[2048,768]{0,1:T(8,128)(2,1)S(1)} %convolution_convert_fusion.2), kind=kLoop, calls=%fused_computation | loop fusion | flops 28311552 | bytes 18874368 | tf_op jit(solution)/shard_map/concatenate | solution.py:75
  180.1 12.4 %copy.46 = bf16[2048,2304]{1,0:T(8,128)(2,1)} copy(bf16[2048,2304]{0,1:T(8,128)(2,1)} %pad_maximum_fusion) | data formatting | bytes 18874368
  192.6 3.9 %fusion.2 = f32[512,2048]{1,0:T(8,128)S(1)} fusion(bf16[512,768]{1,0:T(8,128)(2,1)S(1)} %get-tuple-element.21, bf16[2,2048,768]{2,1,0:T(8,128)(2,1)} %all-gather.8.cloned.1.call-done), kind=kOutput, calls=%fused_computation.10 | convolution fusion | flops 1610612736 | bytes 8126464 | tf_op jit(solution)/shard_map/dot_general | solution.py:14
  196.5 1.9 add_convert_fusion
  198.4 29.7 %all_to_all.46 = bf16[16,32,2048]{2,1,0:T(8,128)(2,1)S(1)} all-to-all(bf16[16,32,2048]{2,1,0:T(8,128)(2,1)S(1)} %bitcast.79), channel_id=1, replica_groups=mesh['dp'=16,'expert'=16] {'expert'}, dimensions={0} | all-to-all | bytes 4194304 | tf_op jit(solution)/shard_map/all_to_all | solution.py:89
  229.3 32.8 %reduce-scatter.4.cloned.1.call-done = bf16[128,2304]{1,0:T(8,128)(2,1)} async-done(((bf16[2048,2304]{1,0:T(8,128)(2,1)}), bf16[128,2304]{1,0:T(8,128)(2,1)}) %reduce-scatter.4.cloned.1.call-update) | async-done | bytes 589840
  (61 shorter events, 12.8 us)
Async XLA Ops:
  7.2 6.4 %copy-start = (bf16[128,2048]{1,0:T(8,128)(2,1)S(1)}, bf16[128,2048]{1,0:T(8,128)(2,1)}, u32[]{:S(2)}) copy-start(bf16[128,2048]{1,0:T(8,128)(2,1)} %param.8) | copy-start | bytes 1572868
  7.2 6.3 %copy-start.5 = (s32[128,2]{0,1:T(2,128)S(1)}, s32[128,2]{0,1:T(2,128)}, u32[]{:S(2)}) copy-start(s32[128,2]{0,1:T(2,128)} %param.10) | copy-start | bytes 3076
  7.2 52.6 %all-gather.14.cloned.1.call-start = ((), (), s32[]{:S(2)}) async-start(), calls=%async_computation.9 | async-start | bytes 3342336 | tf_op jit(solution)/shard_map/all_gather | solution.py:51
  7.9 87.6 %all-gather.12.cloned.1.call-start = ((), (), s32[]{:S(2)}) async-start(), calls=%async_computation.8 | async-start | bytes 3342336 | tf_op jit(solution)/shard_map/all_gather | solution.py:52
  8.7 128.3 %all-gather.10.cloned.1.call-start = ((), (), s32[]{:S(2)}) async-start(), calls=%async_computation.7 | async-start | bytes 3342336 | tf_op jit(solution)/shard_map/all_gather | solution.py:61
  9.4 183.2 %all-gather.8.cloned.1.call-start = ((), (), s32[]{:S(2)}) async-start(), calls=%async_computation.6 | async-start | bytes 6684672 | tf_op jit(solution)/shard_map/all_gather | solution.py:69
  15.6 8.3 %copy-start.4 = (bf16[128,2048]{1,0:T(8,128)(2,1)S(1)}, bf16[128,2048]{1,0:T(8,128)(2,1)}, u32[]{:S(2)}) copy-start(bf16[128,2048]{1,0:T(8,128)(2,1)} %param.9) | copy-start | bytes 1572868
  15.6 34.7 %all-to-all-start.2 = ((bf16[16,32,2048]{2,1,0:T(8,128)(2,1)}), bf16[16,32,2048]{2,1,0:T(8,128)(2,1)S(1)}, u32[]{:S(2)}, u32[]{:S(2)}) async-start(bf16[16,32,2048]{2,1,0:T(8,128)(2,1)} %bitcast.5), calls=%async_computation.2 | async-start | bytes 4194304 | tf_op jit(solution)/shard_map/all_to_all | solution.py:46
  50.4 1.3 copy-start.2
  51.7 49.8 %all-to-all-start.1 = ((bf16[16,32,2048]{2,1,0:T(8,128)(2,1)}), bf16[16,32,2048]{2,1,0:T(8,128)(2,1)S(1)}, u32[]{:S(2)}, u32[]{:S(2)}) async-start(bf16[16,32,2048]{2,1,0:T(8,128)(2,1)} %bitcast.72), calls=%async_computation.1 | async-start | bytes 4194304 | tf_op jit(solution)/shard_map/all_to_all | solution.py:47
  137.0 11.9 %copy-start.8 = (bf16[128,2]{0,1:T(2,128)(2,1)S(1)}, bf16[128,2]{0,1:T(2,128)(2,1)}, u32[]{:S(2)}) copy-start(bf16[128,2]{0,1:T(2,128)(2,1)} %param.11) | copy-start | bytes 1540
  141.5 13.4 %all-to-all-start.4 = ((bf16[16,32,1]{1,2,0:T(2,128)(2,1)}), bf16[16,32,1]{1,2,0:T(2,128)(2,1)S(1)}, u32[]{:S(2)}, u32[]{:S(2)}) async-start(bf16[16,32,1]{1,2,0:T(2,128)(2,1)} %convert_element_type.119), calls=%async_computation.4 | async-start | bytes 16384 | tf_op jit(solution)/shard_map/all_to_all | solution.py:90
  148.8 113.4 %reduce-scatter.4.cloned.1.call-start = ((), (), s32[]{:S(2)}) async-start(), calls=%async_computation.10 | async-start | bytes 10027008
  166.8 2.0 copy-start.7
  166.8 2.4 copy-start.9
  166.9 2.9 %copy-start.10 = (f32[512,768]{1,0:T(8,128)S(1)}, f32[512,768]{1,0:T(8,128)}, u32[]{:S(2)}) copy-start(f32[512,768]{1,0:T(8,128)} %get-tuple-element.23) | copy-start | bytes 4718596
  169.8 2.1 copy-start.3
  192.6 3.9 %copy-start.6 = (bf16[2,2048,768]{2,1,0:T(8,128)(2,1)S(1)}, bf16[2,2048,768]{2,1,0:T(8,128)(2,1)}, u32[]{:S(2)}) copy-start(bf16[2,2048,768]{2,1,0:T(8,128)(2,1)} %all-gather.8.cloned.1.call-done) | copy-start | bytes 18874372
  228.0 36.5 %copy-start.1 = (bf16[128,2048]{1,0:T(8,128)(2,1)S(1)}, bf16[128,2048]{1,0:T(8,128)(2,1)}, u32[]{:S(2)}) copy-start(bf16[128,2048]{1,0:T(8,128)(2,1)} %param.8) | copy-start | bytes 1572868
Sparse Core Ops, SparseCore 0:
  9.9 43.9 all-gather.13
  55.6 39.8 all-gather.11
  97.3 39.5 all-gather.9
  139.2 44.6 all-gather.7
  192.7 69.3 reduce-scatter.3
where the time goes:
time: 272 us; the launch traced here: 271 us
  waiting for transfers between devices  131 us (48%)
  blocking collectives  40.2 us (15%)
  matrix products  34.1 us (13%)
  starting transfers between devices  23.2 us (9%)
  local copies, waits for them, and re-layouts  19.7 us (7%)
  between operations  14.6 us (5%)
  other arithmetic  8.25 us (3%)
    all_gather x1, waiting for transfers between devices, per_device(): piece = lax.all_gather(down_local, 'dp', axis=0, tiled=True)  35.5 us
    unnamed x6, waiting for transfers between devices  34.9 us
    all_gather x1, waiting for transfers between devices, per_device(): lax.all_gather(up_local, 'dp', axis=0, tiled=True)  30.2 us
    all_to_all x1, blocking collectives, per_device(): lax.all_to_all(route_back, 'expert', split_axis=0, concat_axis=0, tiled=T...  29.7 us
    all_to_all x1, waiting for transfers between devices, per_device(): lax.all_to_all(send_rows, 'expert', split_axis=0, concat_axis=0, tiled=True)  24.3 us
    unnamed x26, local copies, waits for them, and re-layouts  18.1 us
    all_to_all x1, blocking collectives, per_device(): lax.all_to_all(send_prob, 'expert', split_axis=0, concat_axis=0, tiled=True)  10.5 us
    dot_general x3, matrix products, contract_last(): lax.dot_general(left, right, (((1,), (1,)), ((), ())), preferred_element_...  9.55 us
  transfers between devices with their start and end apart: 8, of which 5 were waited for; matrix products, arithmetic and copies ran while one was open for 21% of the time, Pallas kernels for 0%

commit v1 on v0

--- a/solution.py
+++ b/solution.py
@@ -58,7 +58,9 @@
     scaled = (prob_in.astype(jnp.float32)[:, None] * grad_in.astype(jnp.float32)).astype(
         jnp.bfloat16
     )
-    piece = lax.all_gather(down_local, "dp", axis=0, tiled=True)
+    piece = jnp.concatenate(
+        lax.all_to_all(jnp.stack([down_local] * lax.axis_size("dp")), "dp", 0, 0), axis=0
+    )
     scaled_part = scaled
     output_part = contract_last(act, piece)
     back_hidden = jnp.dot(scaled_part, piece, preferred_element_type=jnp.float32)

time: 272 us -> 333 us (1.22)
  waiting for transfers between devices: 131 us -> 177 us
  starting transfers between devices: 23.2 us -> 31.9 us
  local copies, waits for them, and re-layouts: 19.7 us -> 23.1 us
    all_to_all x0 -> x1, waiting for transfers between devices: none -> 85.3 us  [per_device(): lax.all_to_all(jnp.stack([down_local] * lax.axis_size('dp')), 'dp', 0, 0)]
    all_gather x1 -> x0, waiting for transfers between devices: 35.5 us -> none  [per_device(): piece = lax.all_gather(down_local, 'dp', axis=0, tiled=True)]
    all_gather x1, waiting for transfers between devices: 30.2 us -> 0.01 us  [per_device(): lax.all_gather(up_local, 'dp', axis=0, tiled=True)]
    all_to_all x1, waiting for transfers between devices: 0.01 us -> 25.8 us  [per_device(): lax.all_to_all(send_grad, 'expert', split_axis=0, concat_axis=0, tiled=True)]
    all_to_all x0 -> x1, starting transfers between devices: none -> 8.61 us  [per_device(): lax.all_to_all(jnp.stack([down_local] * lax.axis_size('dp')), 'dp', 0, 0)]
    unnamed x26 -> x30, local copies, waits for them, and re-layouts: 18.1 us -> 19.6 us
    unnamed x6 -> x5, waiting for transfers between devices: 34.9 us -> 35.2 us
  transfers between devices with their start and end apart: 8 -> 8, of which waited for: 5 -> 5; matrix products, arithmetic and copies ran while one was open for 21% -> 19% of each run, Pallas kernels for 0% -> 0%
where the time goes in v1:
time: 333 us
  waiting for transfers between devices  177 us (53%)
  blocking collectives  41 us (12%)
  matrix products  36.7 us (11%)
  starting transfers between devices  31.9 us (10%)
  local copies, waits for them, and re-layouts  23.1 us (7%)
  between operations  14.7 us (4%)
  other arithmetic  8.27 us (2%)
    all_to_all x1, waiting for transfers between devices, per_device(): lax.all_to_all(jnp.stack([down_local] * lax.axis_size('dp')), 'dp', 0, 0)  85.3 us
    unnamed x5, waiting for transfers between devices  35.2 us
    all_to_all x1, blocking collectives, per_device(): lax.all_to_all(route_back, 'expert', split_axis=0, concat_axis=0, tiled=T...  30.5 us
    all_to_all x1, waiting for transfers between devices, per_device(): lax.all_to_all(send_grad, 'expert', split_axis=0, concat_axis=0, tiled=True)  25.8 us
    all_to_all x1, waiting for transfers between devices, per_device(): lax.all_to_all(send_rows, 'expert', split_axis=0, concat_axis=0, tiled=True)  24.4 us
    unnamed x30, local copies, waits for them, and re-layouts  19.6 us
    all_to_all x1, blocking collectives, per_device(): lax.all_to_all(send_prob, 'expert', split_axis=0, concat_axis=0, tiled=True)  10.6 us
    dot_general x3, matrix products, contract_last(): lax.dot_general(left, right, (((1,), (1,)), ((), ())), preferred_element_...  9.84 us
  transfers between devices with their start and end apart: 8, of which 5 were waited for; matrix products, arithmetic and copies ran while one was open for 19% of the time, Pallas kernels for 0%

profile of v1, /device:TPU:2, one launch (start us, length us, event | category | flops | bytes accessed | tf_op | source)
XLA Modules:
  0.0 332.5 jit_solution(16969919124670220430)
XLA Ops:
  11.6 2.0 convolution_convert_fusion.3
  13.7 7.6 %all-to-all-start.3 = ((bf16[16,32,2048]{2,1,0:T(8,128)(2,1)}), bf16[16,32,2048]{2,1,0:T(8,128)(2,1)S(1)}, u32[]{:S(2)}, u32[]{:S(2)}) async-start(bf16[16,32,2048]{2,1,0:T(8,128)(2,1)} %bitcast.7), calls=%async_computation.3 | async-start | bytes 4194304 | tf_op jit(solution)/shard_map/all_to_all | solution.py:46
  22.0 2.1 convolution_convert_fusion.4
  24.1 24.4 %all-to-all-done.3 = bf16[16,32,2048]{2,1,0:T(8,128)(2,1)S(1)} async-done(((bf16[16,32,2048]{2,1,0:T(8,128)(2,1)}), bf16[16,32,2048]{2,1,0:T(8,128)(2,1)S(1)}, u32[]{:S(2)}, u32[]{:S(2)}) %all-to-all-start.3) | async-done | bytes 2097184 | tf_op jit(solution)/shard_map/all_to_all | solution.py:46
  49.8 8.1 %all-to-all-start.1 = ((bf16[16,32,2048]{2,1,0:T(8,128)(2,1)}), bf16[16,32,2048]{2,1,0:T(8,128)(2,1)S(1)}, u32[]{:S(2)}, u32[]{:S(2)}) async-start(bf16[16,32,2048]{2,1,0:T(8,128)(2,1)} %bitcast.74), calls=%async_computation.1 | async-start | bytes 4194304 | tf_op jit(solution)/shard_map/all_to_all | solution.py:47
  58.8 25.8 %all-to-all-done.1 = bf16[16,32,2048]{2,1,0:T(8,128)(2,1)S(1)} async-done(((bf16[16,32,2048]{2,1,0:T(8,128)(2,1)}), bf16[16,32,2048]{2,1,0:T(8,128)(2,1)S(1)}, u32[]{:S(2)}, u32[]{:S(2)}) %all-to-all-start.1) | async-done | bytes 2097184 | tf_op jit(solution)/shard_map/all_to_all | solution.py:47
  84.5 1.9 stack.6
  86.5 8.6 %all-to-all-start.2 = ((bf16[16,128,768]{2,1,0:T(8,128)(2,1)}), bf16[16,128,768]{2,1,0:T(8,128)(2,1)}, u32[]{:S(2)}, u32[]{:S(2)}) async-start(bf16[16,128,768]{2,1,0:T(8,128)(2,1)} %stack.6), calls=%async_computation.2 | async-start | bytes 6291456 | tf_op jit(solution)/shard_map/all_to_all | solution.py:62
  95.1 5.5 %fusion.5 = f32[512,768]{1,0:T(8,128)} fusion(bf16[512,2048]{1,0:T(8,128)(2,1)} %bitcast.77, bf16[1,2048,768]{2,1,0:T(8,128)(2,1)} %all-gather.10.cloned.1.call-done), kind=kOutput, calls=%fused_computation.15 | convolution fusion | flops 1610612736 | bytes 6815744 | tf_op jit(solution)/shard_map/dot_general | solution.py:54
  100.6 6.2 %multiply_convert_fusion = (bf16[512,768]{1,0:T(8,128)(2,1)}, f32[512,768]{1,0:T(8,128)}) fusion(f32[512,768]{1,0:T(8,128)} %fusion.5, bf16[512,2048]{1,0:T(8,128)(2,1)} %bitcast.78, bf16[1,2048,768]{2,1,0:T(8,128)(2,1)} %all-gather.8.cloned.1.call-done), kind=kOutput, calls=%fused_computation.22 | convolution fusion | flops 1612972032 | bytes 9175040 | tf_op jit(solution)/shard_map/dot_general | solution.py:55
  106.8 85.3 %all-to-all-done.2 = bf16[16,128,768]{2,1,0:T(8,128)(2,1)} async-done(((bf16[16,128,768]{2,1,0:T(8,128)(2,1)}), bf16[16,128,768]{2,1,0:T(8,128)(2,1)}, u32[]{:S(2)}, u32[]{:S(2)}) %all-to-all-start.2) | async-done | bytes 3145760 | tf_op jit(solution)/shard_map/all_to_all | solution.py:62
  192.1 4.1 %fusion.1 = bf16[512]{0:T(512)(128)(2,1)S(1)} fusion(bf16[16,32,2048]{2,1,0:T(8,128)(2,1)S(1)} %all-to-all-done.1, bf16[512,768]{1,0:T(8,128)(2,1)} %get-tuple-element.25, bf16[2048,768]{1,0:T(8,128)(2,1)} %bitcast.6), kind=kOutput, calls=%fused_computation.5 | convolution fusion | flops 1613757952 | bytes 6030336 | tf_op jit(solution)/shard_map/dot_general | solution.py:14
  196.9 7.4 %all-to-all-start.5 = ((bf16[16,32,1]{1,2,0:T(2,128)(2,1)}), bf16[16,32,1]{1,2,0:T(2,128)(2,1)S(1)}, u32[]{:S(2)}, u32[]{:S(2)}) async-start(bf16[16,32,1]{1,2,0:T(2,128)(2,1)} %convert_element_type.139), calls=%async_computation.5 | async-start | bytes 16384 | tf_op jit(solution)/shard_map/all_to_all | solution.py:92
  204.4 6.1 %all-to-all-done.5 = bf16[16,32,1]{1,2,0:T(2,128)(2,1)S(1)} async-done(((bf16[16,32,1]{1,2,0:T(2,128)(2,1)}), bf16[16,32,1]{1,2,0:T(2,128)(2,1)S(1)}, u32[]{:S(2)}, u32[]{:S(2)}) %all-to-all-start.5) | async-done | bytes 1056 | tf_op jit(solution)/shard_map/all_to_all | solution.py:92
  211.4 10.6 %all_to_all.50 = bf16[16,32,1]{1,2,0:T(2,128)(2,1)S(1)} all-to-all(bf16[16,32,1]{1,2,0:T(2,128)(2,1)S(1)} %convert_element_type.138), channel_id=1, replica_groups=mesh['dp'=16,'expert'=16] {'expert'}, dimensions={0} | all-to-all | bytes 2048 | tf_op jit(solution)/shard_map/all_to_all | solution.py:48
  223.2 1.9 convolution_convert_fusion
  227.0 4.2 %multiply_convert_fusion.2 = (bf16[512,768]{1,0:T(8,128)(2,1)S(1)}, bf16[512,768]{1,0:T(8,128)(2,1)S(1)}) fusion(f32[512,768]{1,0:T(8,128)S(1)} %copy-done.10, f32[512,768]{1,0:T(8,128)S(1)} %copy-done.12, bf16[512,2048]{1,0:T(8,128)(2,1)S(1)} %bitcast.81, bf16[2048,768]{1,0:T(8,128)(2,1)} %bitcast.6), kind=kOutput, calls=%fused_computation.24 | convolution fusion | flops 1615724544 | bytes 9961472 | tf_op jit(solution)/shard_map/dot_general | solution.py:66
  231.2 1.9 convolution_convert_fusion.1
  233.0 1.9 convolution_convert_fusion.2
  234.9 4.4 %pad_maximum_fusion = bf16[2048,2304]{0,1:T(8,128)(2,1)} fusion(bf16[2048,768]{0,1:T(8,128)(2,1)S(1)} %convolution_convert_fusion, bf16[2048,768]{0,1:T(8,128)(2,1)S(1)} %convolution_convert_fusion.1, bf16[2048,768]{0,1:T(8,128)(2,1)S(1)} %convolution_convert_fusion.2), kind=kLoop, calls=%fused_computation | loop fusion | flops 28311552 | bytes 18874368 | tf_op jit(solution)/shard_map/concatenate | solution.py:77
  239.4 12.8 %copy.54 = bf16[2048,2304]{1,0:T(8,128)(2,1)} copy(bf16[2048,2304]{0,1:T(8,128)(2,1)} %pad_maximum_fusion) | data formatting | bytes 18874368
  252.2 3.9 %fusion.3 = f32[512,2048]{1,0:T(8,128)S(1)} fusion(bf16[512,768]{1,0:T(8,128)(2,1)S(1)} %get-tuple-element.24, bf16[2,2048,768]{2,1,0:T(8,128)(2,1)} %all-gather.6.cloned.1.call-done), kind=kOutput, calls=%fused_computation.12 | convolution fusion | flops 1610612736 | bytes 8126464 | tf_op jit(solution)/shard_map/dot_general | solution.py:14
  258.0 30.5 %all_to_all.51 = bf16[16,32,2048]{2,1,0:T(8,128)(2,1)S(1)} all-to-all(bf16[16,32,2048]{2,1,0:T(8,128)(2,1)S(1)} %bitcast.82), channel_id=1, replica_groups=mesh['dp'=16,'expert'=16] {'expert'}, dimensions={0} | all-to-all | bytes 4194304 | tf_op jit(solution)/shard_map/all_to_all | solution.py:91
  289.7 33.8 %reduce-scatter.4.cloned.1.call-done = bf16[128,2304]{1,0:T(8,128)(2,1)} async-done(((bf16[2048,2304]{1,0:T(8,128)(2,1)}), bf16[128,2304]{1,0:T(8,128)(2,1)}) %reduce-scatter.4.cloned.1.call-update) | async-done | bytes 589840
  (67 shorter events, 16.9 us)
Async XLA Ops:
  7.2 4.5 %copy-start = (bf16[128,2048]{1,0:T(8,128)(2,1)S(1)}, bf16[128,2048]{1,0:T(8,128)(2,1)}, u32[]{:S(2)}) copy-start(bf16[128,2048]{1,0:T(8,128)(2,1)} %param.8) | copy-start | bytes 1572868
  7.2 87.9 %all-gather.10.cloned.1.call-start = ((), (), s32[]{:S(2)}) async-start(), calls=%async_computation.9 | async-start | bytes 3342336 | tf_op jit(solution)/shard_map/all_gather | solution.py:51
  7.9 92.7 %all-gather.8.cloned.1.call-start = ((), (), s32[]{:S(2)}) async-start(), calls=%async_computation.8 | async-start | bytes 3342336 | tf_op jit(solution)/shard_map/all_gather | solution.py:52
  13.7 8.3 %copy-start.6 = (bf16[128,2048]{1,0:T(8,128)(2,1)S(1)}, bf16[128,2048]{1,0:T(8,128)(2,1)}, u32[]{:S(2)}) copy-start(bf16[128,2048]{1,0:T(8,128)(2,1)} %param.9) | copy-start | bytes 1572868
  13.7 34.7 %all-to-all-start.3 = ((bf16[16,32,2048]{2,1,0:T(8,128)(2,1)}), bf16[16,32,2048]{2,1,0:T(8,128)(2,1)S(1)}, u32[]{:S(2)}, u32[]{:S(2)}) async-start(bf16[16,32,2048]{2,1,0:T(8,128)(2,1)} %bitcast.7), calls=%async_computation.3 | async-start | bytes 4194304 | tf_op jit(solution)/shard_map/all_to_all | solution.py:46
  48.4 1.3 copy-start.2
  48.4 9.5 %copy-start.4 = (bf16[1,128,768]{2,1,0:T(8,128)(2,1)S(1)}, bf16[1,128,768]{2,1,0:T(8,128)(2,1)}, u32[]{:S(2)}) copy-start(bf16[1,128,768]{2,1,0:T(8,128)(2,1)} %param.13) | copy-start | bytes 589828
  48.4 9.5 %copy-start.5 = (bf16[1,128,768]{2,1,0:T(8,128)(2,1)S(1)}, bf16[1,128,768]{2,1,0:T(8,128)(2,1)}, u32[]{:S(2)}) copy-start(bf16[1,128,768]{2,1,0:T(8,128)(2,1)} %param.14) | copy-start | bytes 589828
  48.4 36.1 %copy-start.7 = (bf16[1,128,768]{2,1,0:T(8,128)(2,1)S(1)}, bf16[1,128,768]{2,1,0:T(8,128)(2,1)}, u32[]{:S(2)}) copy-start(bf16[1,128,768]{2,1,0:T(8,128)(2,1)} %param.15) | copy-start | bytes 589828
  49.8 34.8 %all-to-all-start.1 = ((bf16[16,32,2048]{2,1,0:T(8,128)(2,1)}), bf16[16,32,2048]{2,1,0:T(8,128)(2,1)S(1)}, u32[]{:S(2)}, u32[]{:S(2)}) async-start(bf16[16,32,2048]{2,1,0:T(8,128)(2,1)} %bitcast.74), calls=%async_computation.1 | async-start | bytes 4194304 | tf_op jit(solution)/shard_map/all_to_all | solution.py:47
  57.9 194.3 %all-gather.6.cloned.1.call-start = ((), (), s32[]{:S(2)}) async-start(), calls=%async_computation.7 | async-start | bytes 6684672 | tf_op jit(solution)/shard_map/all_gather | solution.py:71
  86.5 105.6 %all-to-all-start.2 = ((bf16[16,128,768]{2,1,0:T(8,128)(2,1)}), bf16[16,128,768]{2,1,0:T(8,128)(2,1)}, u32[]{:S(2)}, u32[]{:S(2)}) async-start(bf16[16,128,768]{2,1,0:T(8,128)(2,1)} %stack.6), calls=%async_computation.2 | async-start | bytes 6291456 | tf_op jit(solution)/shard_map/all_to_all | solution.py:62
  192.1 12.2 %copy-start.9 = (bf16[128,2]{0,1:T(2,128)(2,1)S(1)}, bf16[128,2]{0,1:T(2,128)(2,1)}, u32[]{:S(2)}) copy-start(bf16[128,2]{0,1:T(2,128)(2,1)} %param.11) | copy-start | bytes 1540
  196.9 13.6 %all-to-all-start.5 = ((bf16[16,32,1]{1,2,0:T(2,128)(2,1)}), bf16[16,32,1]{1,2,0:T(2,128)(2,1)S(1)}, u32[]{:S(2)}, u32[]{:S(2)}) async-start(bf16[16,32,1]{1,2,0:T(2,128)(2,1)} %convert_element_type.139), calls=%async_computation.5 | async-start | bytes 16384 | tf_op jit(solution)/shard_map/all_to_all | solution.py:92
  204.3 119.2 %reduce-scatter.4.cloned.1.call-start = ((), (), s32[]{:S(2)}) async-start(), calls=%async_computation.10 | async-start | bytes 10027008
  222.1 1.1 copy-start.11
  225.1 1.4 copy-start.10
  225.1 1.9 copy-start.12
  227.0 4.2 %copy-start.3 = (bf16[16,32,2048]{2,1,0:T(8,128)(2,1)S(1)}, bf16[16,32,2048]{2,1,0:T(8,128)(2,1)}, u32[]{:S(2)}) copy-start(bf16[16,32,2048]{2,1,0:T(8,128)(2,1)} %copy-done.2) | copy-start | bytes 6291460
  252.2 3.9 %copy-start.8 = (bf16[2,2048,768]{2,1,0:T(8,128)(2,1)S(1)}, bf16[2,2048,768]{2,1,0:T(8,128)(2,1)}, u32[]{:S(2)}) copy-start(bf16[2,2048,768]{2,1,0:T(8,128)(2,1)} %all-gather.6.cloned.1.call-done) | copy-start | bytes 18874372
  288.4 37.5 %copy-start.1 = (bf16[128,2048]{1,0:T(8,128)(2,1)S(1)}, bf16[128,2048]{1,0:T(8,128)(2,1)}, u32[]{:S(2)}) copy-start(bf16[128,2048]{1,0:T(8,128)(2,1)} %param.8) | copy-start | bytes 1572868
Sparse Core Ops, SparseCore 0:
  9.8 44.0 all-gather.9
  55.7 39.6 all-gather.7
  97.9 100.0 all-gather.5
  252.3 71.1 reduce-scatter.3
